TPU v7x, 32 devices: a whole 2x2x4 slice. The times are simulated.
32 devices in a mesh: band: 8 (over z, y), tok: 4 (over x, core).
Axes of the slice: x: 2, y: 2, z: 4, core: 2. Of those that a mesh axis runs over, the one named last changes fastest.
Arguments:
- pixels: bfloat16 [4, 8, 32, 256, 256], P('tok', None, 'band'), may hold values from -6 to 6
- wave_table: float32 [64], replicated, may hold values from 0.4 to 12
- wave_index: int32 [4, 8, 32], P('tok'), may hold values from 0 to 63
- patch_count: int32 [4, 8], P('tok', 'band'), may hold values from 49 to 256, as said below
- d_out: bfloat16 [4, 8, 256, 768], P('tok', 'band'), may hold values from -6 to 6
- gen_w: bfloat16 [196608, 128], P(('band', 'tok')), may hold values from -0.5 to 0.5
- gen_b: float32 [128, 768], replicated, may hold values from -0.25 to 0.25
- bias_token: float32 [128], replicated, may hold values from -6 to 6
- hyper_query: float32 [128, 128], replicated, may hold values from -1 to 1
- hyper_key: float32 [128, 128], replicated, may hold values from -1 to 1
- hyper_value: float32 [128, 128], replicated, may hold values from -0.5 to 0.5
- hyper_out: float32 [128, 128], replicated, may hold values from -0.5 to 0.5
- hyper_up: float32 [128, 2048], replicated, may hold values from -0.5 to 0.5
- hyper_down: float32 [2048, 128], replicated, may hold values from -0.125 to 0.125
- hyper_gain1: float32 [128], replicated, may hold values from 0.1 to 1.9
- hyper_gain2: float32 [128], replicated, may hold values from 0.1 to 1.9
- w_qkv: bfloat16 [768, 2304], P(None, 'tok'), may hold values from -0.21875 to 0.21875
- w_out: bfloat16 [768, 768], P(None, 'tok'), may hold values from -1.75 to 1.75
- w_up: bfloat16 [768, 3072], P(None, 'tok'), may hold values from -0.21875 to 0.21875
- w_down: bfloat16 [3072, 768], P('tok'), may hold values from -0.109375 to 0.109375
- ln1_gain: float32 [768], replicated, may hold values from 0.5 to 1.5
- ln2_gain: float32 [768], replicated, may hold values from 0.5 to 1.5
Outputs:
- layer_out: bfloat16 [4, 8, 256, 768], P('tok', 'band')
- pixel_grad: bfloat16 [4, 8, 32, 256, 256], P('tok', None, 'band')
- grad_gen_w: float32 [196608, 128], P(('band', 'tok'))
- grad_gen_b: float32 [128, 768], replicated
- grad_bias_token: float32 [128], replicated
- grad_hyper_query: float32 [128, 128], replicated
- grad_hyper_key: float32 [128, 128], replicated
- grad_hyper_value: float32 [128, 128], replicated
- grad_hyper_out: float32 [128, 128], replicated
- grad_hyper_up: float32 [128, 2048], replicated
- grad_hyper_down: float32 [2048, 128], replicated
- grad_hyper_gain1: float32 [128], replicated
- grad_hyper_gain2: float32 [128], replicated
- grad_w_qkv: float32 [768, 2304], P(None, ('band', 'tok'))
- grad_w_out: float32 [768, 768], P(None, ('band', 'tok'))
- grad_w_up: float32 [768, 3072], P(None, ('band', 'tok'))
- grad_w_down: float32 [3072, 768], P(('band', 'tok'))
- grad_ln1_gain: float32 [768], P(('band', 'tok'))
- grad_ln2_gain: float32 [768], P(('band', 'tok'))
Inputs may be any that keep to these rules, and one draw needn't show every extreme that they name: `patch_count`: each entry is 49, 196 or 256; every draw has an image with 49 and one with 256.
All inputs are finite; a program needn't handle non-finite values.
Results may differ from a plain program's by a relative error of at most 0.028.
Values may be sent and summed in bfloat16 or wider, within the bound.
A program may use at most 384 MiB of HBM per device.

v0:
```python
import math
import jax
import jax.numpy as jnp
from jax import lax
from jax.sharding import PartitionSpec as P

HD = 64
HHEADS = 4
EPS_BLOCK = 1e-06
EPS_HYPER = 1e-05
PRECISE = lax.Precision.HIGHEST


def layer_norm(values, scaling, epsilon):
    center = values - jnp.mean(values, axis=-1, keepdims=True)
    spread = jnp.mean(center * center, axis=-1, keepdims=True)
    return center * lax.rsqrt(spread + epsilon) * scaling


def block_norm(values, scaling):
    return layer_norm(values, scaling, EPS_BLOCK)


def exact_gelu(values):
    return jax.nn.gelu(values, approximate=False)


def wave_features(lengths, model_dim):
    middle = model_dim // 2
    angular = 1.0 / 10000.0 ** (jnp.arange(middle, dtype=jnp.float32) / middle)
    phases = (100.0 * lengths)[..., None] * angular
    return jnp.concatenate([jnp.sin(phases), jnp.cos(phases)], axis=-1)


def hyper_layer(features, params):
    (
        bias_token,
        hyper_query,
        hyper_key,
        hyper_value,
        hyper_out,
        hyper_up,
        hyper_down,
        hyper_gain1,
        hyper_gain2,
    ) = params
    images = features.shape[0]
    model_dim = features.shape[-1]
    head_size = model_dim // HHEADS
    tokens = jnp.concatenate(
        [features, jnp.broadcast_to(bias_token, (images, 1, model_dim))], axis=1
    )
    length = tokens.shape[1]
    queries = jnp.einsum("nsc,ce->nse", tokens, hyper_query, precision=PRECISE).reshape(
        images, length, HHEADS, head_size
    )
    keys_all = jnp.einsum("nsc,ce->nse", tokens, hyper_key, precision=PRECISE).reshape(
        images, length, HHEADS, head_size
    )
    values_all = jnp.einsum("nsc,ce->nse", tokens, hyper_value, precision=PRECISE).reshape(
        images, length, HHEADS, head_size
    )
    scores = jnp.einsum("nshe,nthe->nhst", queries, keys_all, precision=PRECISE) / math.sqrt(
        head_size
    )
    weights = jax.nn.softmax(scores, axis=-1)
    blended = jnp.einsum("nhst,nthe->nshe", weights, values_all, precision=PRECISE).reshape(
        images, length, model_dim
    )
    segment_one = layer_norm(
        tokens + jnp.einsum("nse,ef->nsf", blended, hyper_out, precision=PRECISE),
        hyper_gain1,
        EPS_HYPER,
    )
    expanded = jax.nn.gelu(
        jnp.einsum("nse,ef->nsf", segment_one, hyper_up, precision=PRECISE), approximate=False
    )
    second = layer_norm(
        segment_one + jnp.einsum("nsf,fe->nse", expanded, hyper_down, precision=PRECISE),
        hyper_gain2,
        EPS_HYPER,
    )
    return (second[:, :-1, :], second[:, -1, :])


def contract_rows(left_side, right_side):
    return lax.dot_general(
        left_side, right_side, (((0,), (0,)), ((), ())), preferred_element_type=jnp.float32
    )


def contract_cols(left_side, right_side):
    return lax.dot_general(
        left_side, right_side, (((1,), (1,)), ((), ())), preferred_element_type=jnp.float32
    )


def attention_scores(queries, keys_low, usable):
    head_size = queries.shape[-1]
    scores = jnp.einsum(
        "iqhe,ikhe->ihqk", queries, keys_low, preferred_element_type=jnp.float32
    ) / math.sqrt(head_size)
    return jnp.where(usable[:, None, None, :], scores, -1e30)


def block_forward(embedded, usable, weights_full, ln1_gain, ln2_gain):
    w_qkv_full, w_out_full, w_up_full, w_down_full = weights_full
    images, slot_count, model_dim = embedded.shape
    row_count = images * slot_count
    head_count = model_dim // HD
    flat_rows = embedded.reshape(row_count, model_dim)
    normed_one = block_norm(flat_rows, ln1_gain).astype(jnp.bfloat16)
    qkv_low = jnp.dot(normed_one, w_qkv_full, preferred_element_type=jnp.float32).astype(
        jnp.bfloat16
    )
    sections = qkv_low.reshape(images, slot_count, 3, head_count, HD)
    queries = sections[:, :, 0]
    keys_low = sections[:, :, 1]
    values_low = sections[:, :, 2]
    scores = attention_scores(queries, keys_low, usable)
    highest = jnp.max(scores, axis=-1, keepdims=True)
    lifted = jnp.exp(scores - highest)
    totals = jnp.sum(lifted, axis=-1, keepdims=True)
    attn_probs = (lifted / totals).astype(jnp.bfloat16)
    log_mass = highest + jnp.log(totals)
    attended = (
        jnp.einsum("ihqk,ikhe->iqhe", attn_probs, values_low, preferred_element_type=jnp.float32)
        .astype(jnp.bfloat16)
        .reshape(row_count, model_dim)
    )
    middle = flat_rows + jnp.dot(attended, w_out_full, preferred_element_type=jnp.float32)
    normed_two = block_norm(middle, ln2_gain).astype(jnp.bfloat16)
    hidden = jnp.dot(normed_two, w_up_full, preferred_element_type=jnp.float32)
    active = exact_gelu(hidden).astype(jnp.bfloat16)
    output = middle + jnp.dot(active, w_down_full, preferred_element_type=jnp.float32)
    return (
        flat_rows,
        normed_one,
        queries,
        keys_low,
        values_low,
        log_mass,
        attended,
        middle,
        normed_two,
        hidden,
        active,
        output,
    )


def block_backward(stored, usable, grad_rows, weights_full, ln1_gain, ln2_gain):
    (
        flat_rows,
        normed_one,
        queries,
        keys_low,
        values_low,
        log_mass,
        attended,
        middle,
        normed_two,
        hidden,
        active,
        output,
    ) = stored
    w_qkv_full, w_out_full, w_up_full, w_down_full = weights_full
    images, slot_count, head_count, head_size = queries.shape
    row_count, model_dim = flat_rows.shape
    grad_low = grad_rows.astype(jnp.bfloat16)
    grad_down = contract_rows(active, grad_low)
    d_active = contract_cols(grad_low, w_down_full)
    gelu_back = jax.vjp(exact_gelu, hidden)[1]
    d_hidden = gelu_back(d_active)[0].astype(jnp.bfloat16)
    grad_up_turned = contract_rows(d_hidden, normed_two)
    d_normed_two = contract_cols(d_hidden, w_up_full)
    norm_back_two = jax.vjp(block_norm, middle, ln2_gain)[1]
    d_middle_norm, grad_gain_two = norm_back_two(d_normed_two)
    d_middle = grad_rows + d_middle_norm
    d_middle_low = d_middle.astype(jnp.bfloat16)
    grad_out_turned = contract_rows(d_middle_low, attended)
    d_attended = (
        contract_cols(d_middle_low, w_out_full)
        .astype(jnp.bfloat16)
        .reshape(images, slot_count, head_count, head_size)
    )
    scores = attention_scores(queries, keys_low, usable)
    attn_float = jnp.exp(scores - log_mass)
    attn_probs = attn_float.astype(jnp.bfloat16)
    d_values = jnp.einsum(
        "ihqk,iqhe->ikhe", attn_probs, d_attended, preferred_element_type=jnp.float32
    ).astype(jnp.bfloat16)
    d_probs = jnp.einsum(
        "iqhe,ikhe->ihqk", d_attended, values_low, preferred_element_type=jnp.float32
    )
    d_scores = (
        attn_float * (d_probs - jnp.sum(attn_float * d_probs, axis=-1, keepdims=True))
    ).astype(jnp.bfloat16)
    d_queries = (
        jnp.einsum("ihqk,ikhe->iqhe", d_scores, keys_low, preferred_element_type=jnp.float32)
        / math.sqrt(head_size)
    ).astype(jnp.bfloat16)
    d_keys = (
        jnp.einsum("ihqk,iqhe->ikhe", d_scores, queries, preferred_element_type=jnp.float32)
        / math.sqrt(head_size)
    ).astype(jnp.bfloat16)
    d_qkv = jnp.stack([d_queries, d_keys, d_values], axis=2).reshape(row_count, 3 * model_dim)
    grad_qkv_turned = contract_rows(d_qkv, normed_one)
    d_normed_one = contract_cols(d_qkv, w_qkv_full)
    norm_back_one = jax.vjp(block_norm, flat_rows, ln1_gain)[1]
    d_flat, grad_gain_one = norm_back_one(d_normed_one)
    return (
        d_middle + d_flat,
        (grad_qkv_turned, grad_out_turned, grad_up_turned, grad_down, grad_gain_one, grad_gain_two),
    )


def body(
    pixels,
    wave_table,
    wave_index,
    patch_count,
    d_out,
    gen_w,
    gen_b,
    bias_token,
    hyper_query,
    hyper_key,
    hyper_value,
    hyper_out,
    hyper_up,
    hyper_down,
    hyper_gain1,
    hyper_gain2,
    w_qkv,
    w_out,
    w_up,
    w_down,
    ln1_gain,
    ln2_gain,
):
    group_images = pixels.shape[1]
    band_share = pixels.shape[2]
    slot_count = pixels.shape[3]
    pixel_count = pixels.shape[4]
    own_images = patch_count.shape[1]
    model_dim = w_out.shape[0]
    hyper_dim = gen_w.shape[1]
    all_bands = wave_index.shape[2]
    factor = 1.0 / math.sqrt(all_bands * pixel_count)
    band_place = lax.axis_index("band")
    hyper_params = (
        bias_token,
        hyper_query,
        hyper_key,
        hyper_value,
        hyper_out,
        hyper_up,
        hyper_down,
        hyper_gain1,
        hyper_gain2,
    )
    catalog = lax.broadcasted_iota(jnp.int32, (1, 1, wave_table.shape[0]), 2)
    picked = (wave_index[0][:, :, None] == catalog).astype(jnp.float32)
    lengths_all = jnp.sum(picked * wave_table, axis=-1)
    weights_full = (
        lax.all_gather(w_qkv, "tok", axis=1, tiled=True),
        lax.all_gather(w_out, "tok", axis=1, tiled=True),
        lax.all_gather(w_up, "tok", axis=1, tiled=True),
        lax.all_gather(w_down, "tok", axis=0, tiled=True),
    )
    hyper_input = wave_features(lengths_all, hyper_dim)

    def run_hyper(params):
        return hyper_layer(hyper_input, params)

    (band_feats, bias_feats), hyper_back = jax.vjp(run_hyper, hyper_params)
    band_low = (
        lax.dynamic_slice_in_dim(band_feats, band_place * band_share, band_share, 1)
        .astype(jnp.bfloat16)
        .reshape(-1, hyper_dim)
    )
    bias_own = lax.dynamic_slice_in_dim(bias_feats, band_place * own_images, own_images, 0)
    gen_full = lax.all_gather(gen_w, ("band", "tok"), axis=0, tiled=True)
    kernels = (contract_cols(band_low, gen_full) * factor).astype(jnp.bfloat16)
    kernel_grid = kernels.reshape(group_images, band_share, pixel_count, model_dim)
    pixel_part = pixels[0]
    product = jnp.einsum(
        "ibsp,ibpd->isd", pixel_part, kernel_grid, preferred_element_type=jnp.float32
    )
    convolved = lax.psum_scatter(
        product.reshape(own_images * slot_count * lax.axis_size("band"), model_dim).astype(
            jnp.bfloat16
        ),
        "band",
        scatter_dimension=0,
        tiled=True,
    ).astype(jnp.float32)
    bias_rows = jnp.dot(bias_own, gen_b, precision=PRECISE)
    embedded = convolved.reshape(own_images, slot_count, model_dim) + bias_rows[:, None, :]
    usable = lax.broadcasted_iota(jnp.int32, (own_images, slot_count), 1) < patch_count[0][:, None]
    stored = block_forward(embedded, usable, weights_full, ln1_gain, ln2_gain)
    row_mask = usable.reshape(-1, 1)
    layer_out = (
        jnp.where(row_mask, stored[-1], 0.0)
        .astype(jnp.bfloat16)
        .reshape(1, own_images, slot_count, model_dim)
    )
    stored = block_forward(
        lax.optimization_barrier(embedded), usable, weights_full, ln1_gain, ln2_gain
    )
    grad_rows = jnp.where(row_mask, d_out[0].reshape(-1, model_dim).astype(jnp.float32), 0.0)
    d_embed, block_terms = block_backward(
        stored, usable, grad_rows, weights_full, ln1_gain, ln2_gain
    )
    d_embed_low = d_embed.astype(jnp.bfloat16).reshape(own_images, slot_count, model_dim)
    d_bias = jnp.sum(d_embed.reshape(own_images, slot_count, model_dim), axis=1)
    d_bias_feat = jnp.dot(d_bias, gen_b.T, precision=PRECISE)
    grad_gen_b = jnp.dot(bias_own.T, d_bias, precision=PRECISE)
    d_gathered = lax.all_gather(d_embed_low, "band", axis=0, tiled=True)
    pixel_grad = jnp.einsum(
        "isd,ibpd->ibsp", d_gathered, kernel_grid, preferred_element_type=jnp.float32
    ).astype(jnp.bfloat16)[None]
    d_kernel = (
        jnp.einsum("ibsp,isd->ibpd", pixels[0], d_gathered, preferred_element_type=jnp.float32)
        .astype(jnp.bfloat16)
        .reshape(-1, pixel_count * model_dim)
    )
    d_band_local = jnp.dot(d_kernel, gen_full, preferred_element_type=jnp.float32) * factor
    grad_gen_w = lax.psum_scatter(
        contract_rows(d_kernel, band_low) * factor, ("band", "tok"), scatter_dimension=0, tiled=True
    )
    d_band_own = d_band_local.reshape(group_images, band_share, hyper_dim)
    d_band = lax.dynamic_update_slice_in_dim(
        jnp.zeros(band_feats.shape, jnp.float32), d_band_own, band_place * band_share, 1
    )
    d_bias_all = lax.dynamic_update_slice_in_dim(
        jnp.zeros(bias_feats.shape, jnp.float32), d_bias_feat, band_place * own_images, 0
    )
    (
        grad_token,
        grad_query,
        grad_key,
        grad_value,
        grad_mix,
        grad_expand,
        grad_shrink,
        grad_first_gain,
        grad_second_gain,
    ) = hyper_back((d_band, d_bias_all))[0]
    qkv_turned, out_turned, up_turned, grad_down, gain_one, gain_two = block_terms
    block_sums = (
        lax.psum_scatter(qkv_turned, ("band", "tok"), scatter_dimension=0, tiled=True),
        lax.psum_scatter(out_turned, ("band", "tok"), scatter_dimension=0, tiled=True),
        lax.psum_scatter(up_turned, ("band", "tok"), scatter_dimension=0, tiled=True),
        lax.psum_scatter(grad_down, ("band", "tok"), scatter_dimension=0, tiled=True),
        lax.psum_scatter(gain_one, ("band", "tok"), scatter_dimension=0, tiled=True),
        lax.psum_scatter(gain_two, ("band", "tok"), scatter_dimension=0, tiled=True),
    )
    hyper_sums = lax.psum(
        (
            grad_token,
            grad_query,
            grad_key,
            grad_value,
            grad_mix,
            grad_expand,
            grad_shrink,
            grad_first_gain,
            grad_second_gain,
            grad_gen_b,
        ),
        ("band", "tok"),
    )
    return (
        layer_out,
        pixel_grad,
        grad_gen_w,
        hyper_sums[9],
        hyper_sums[0],
        hyper_sums[1],
        hyper_sums[2],
        hyper_sums[3],
        hyper_sums[4],
        hyper_sums[5],
        hyper_sums[6],
        hyper_sums[7],
        hyper_sums[8],
        block_sums[0].T,
        block_sums[1].T,
        block_sums[2].T,
        block_sums[3],
        block_sums[4],
        block_sums[5],
    )


def solution(mesh):
    placed = (
        P("tok", None, "band", None, None),
        P(),
        P("tok", None, None),
        P("tok", "band"),
        P("tok", "band", None, None),
        P(("band", "tok"), None),
        P(),
        P(),
        P(),
        P(),
        P(),
        P(),
        P(),
        P(),
        P(),
        P(),
        P(None, "tok"),
        P(None, "tok"),
        P(None, "tok"),
        P("tok", None),
        P(),
        P(),
    )
    return jax.shard_map(
        body,
        mesh=mesh,
        in_specs=placed,
        out_specs=(
            P("tok", "band", None, None),
            P("tok", None, "band", None, None),
            P(("band", "tok"), None),
            P(),
            P(),
            P(),
            P(),
            P(),
            P(),
            P(),
            P(),
            P(),
            P(),
            P(None, ("band", "tok")),
            P(None, ("band", "tok")),
            P(None, ("band", "tok")),
            P(("band", "tok"), None),
            P(("band", "tok")),
            P(("band", "tok")),
        ),
        check_vma=False,
    )
```

profile of v0, /device:TPU:0, one launch (start us, length us, event | category | flops | bytes accessed | tf_op | source)
XLA Modules:
  0.0 2059.1 jit_solution(18307944858478254983)
XLA Ops:
  17.6 3.6 fusion.80
  21.3 6.0 fusion.22
  27.3 2.4 fusion.203
  30.2 259.9 %all-gather.8.cloned.1.call-done = bf16[196608,128]{1,0:T(8,128)(2,1)} async-done(((bf16[6144,128]{1,0:T(8,128)(2,1)}), bf16[196608,128]{1,0:T(8,128)(2,1)}) %all-gather.8.cloned.1.call-update) | async-done | bytes 50331664 | tf_op jit(solution)/shard_map/all_gather | solution.py:284
  290.0 25.9 %fusion.1 = bf16[32,196608]{1,0:T(8,128)(2,1)} fusion(bf16[32,128]{1,0:T(8,128)(2,1)S(1)} %bitcast.310, bf16[196608,128]{1,0:T(8,128)(2,1)} %all-gather.8.cloned.1.call-done), kind=kOutput, calls=%fused_computation.3 | convolution fusion | flops 1623195648 | bytes 62922752 | tf_op jit(solution)/shard_map/dot_general | solution.py:93
  315.9 8.2 copy.211
  324.1 5.7 bitcast_convert_fusion
  333.5 69.1 %reduce-scatter.7.cloned.1.call-done = bf16[256,768]{1,0:T(8,128)(2,1)} async-done(((bf16[2048,768]{1,0:T(8,128)(2,1)}), bf16[256,768]{1,0:T(8,128)(2,1)}) %reduce-scatter.7.cloned.1.call-update) | async-done | bytes 393232 | tf_op jit(solution)/shard_map/reduce_scatter | solution.py:291
  403.8 1.8 fusion.76
  406.0 4.2 convolution_convert_fusion
  410.2 2.9 copy.155
  413.1 1.9 fusion.206
  418.5 2.0 fusion.207
  422.2 5.5 fusion.195
  427.7 29.5 %all-gather.16.cloned.1.call-done = bf16[3072,768]{1,0:T(8,128)(2,1)} async-done(((bf16[768,768]{1,0:T(8,128)(2,1)}), bf16[3072,768]{1,0:T(8,128)(2,1)}) %all-gather.16.cloned.1.call-update) | async-done | bytes 4718608 | tf_op jit(solution)/shard_map/all_gather | solution.py:270
  457.3 10.8 add_convert_fusion
  468.1 2.3 multiply_reduce_fusion.1
  473.1 1.9 copy.157
  475.0 2.8 fusion.62
  478.0 1.8 multiply_reduce_fusion
  483.2 1.9 multiply_reduce_fusion.2
  491.4 2.9 fusion.208
  495.9 51.9 %all-gather.18.cloned.1.call-done = bf16[2048,768]{1,0:T(8,128)(2,1)} async-done(((bf16[256,768]{1,0:T(8,128)(2,1)}), bf16[2048,768]{1,0:T(8,128)(2,1)}) %all-gather.18.cloned.1.call-update) | async-done | bytes 3145744 | tf_op jit(solution)/shard_map/all_gather | solution.py:320
  547.8 11.1 convert_bitcast_fusion
  558.8 16.8 copy.212
  575.6 23.0 %convolution_multiply_fusion.5 = f32[32,128]{1,0:T(8,128)S(1)} fusion(bf16[32,196608]{1,0:T(8,128)(2,1)} %bitcast.272, bf16[196608,128]{1,0:T(8,128)(2,1)} %all-gather.8.cloned.1.call-done), kind=kOutput, calls=%fused_computation.123 | convolution fusion | flops 1610616832 | bytes 62930944 | tf_op jit(solution)/shard_map/dot_general | solution.py:329
  599.8 4.6 multiply_add_fusion
  605.8 2.4 multiply_reduce_fusion.12
  611.2 2.7 multiply_reduce_fusion.9
  613.9 2.3 convolution_bitcast_fusion.2
  625.6 3.2 convolution_bitcast_fusion.1
  628.8 6.3 convolution_bitcast_fusion
  635.2 5.4 fusion.87
  641.6 11.6 fusion.34
  653.9 6.6 fusion.194
  661.3 39.6 %convolution_multiply_fusion = f32[196608,128]{1,0:T(8,128)} fusion(bf16[32,196608]{1,0:T(8,128)(2,1)} %bitcast.273, bf16[32,128]{1,0:T(8,128)(2,1)S(1)} %bitcast.311), kind=kOutput, calls=%fused_computation.1 | convolution fusion | flops 1635778560 | bytes 113254400 | tf_op jit(solution)/shard_map/dot_general | solution.py:87
  701.9 3.2 convolution_convert_fusion.1
  710.2 13.5 fusion.65
  723.7 11.1 convert_bitcast_fusion.1
  734.9 6.6 copy.179
  745.3 39.6 %all-reduce.4 = (f32[128]{0:T(128)}, f32[128]{0:T(128)}, f32[128]{0:T(128)}, f32[768]{0:T(1024)S(1)}, f32[768]{0:T(1024)S(1)}) all-reduce(f32[128]{0:T(128)S(1)} %fusion.148, f32[128]{0:T(128)S(1)} %copy-done.107, f32[128]{0:T(128)S(1)} %copy-done.106, f32[768]{0:T(1024)S(1)} %copy-done.105, ...), channel_id=1, replica_groups=mesh['band'=8,'tok'=4] {'band','tok'}, use_global_device_ids=true, to_apply=%region_34.35 | all-reduce | flops 1920 | bytes 15360 | tf_op jit(solution)/shard_map/psum | solution.py:360
  786.1 12.8 all-reduce.8.cloned.1.call-done
  798.9 124.6 %reduce-scatter.11.cloned.1.call-done = f32[72,768]{1,0:T(8,128)} async-done(((f32[2304,768]{1,0:T(8,128)}), f32[72,768]{1,0:T(8,128)}) %reduce-scatter.11.cloned.1.call-update) | async-done | bytes 221200 | tf_op jit(solution)/shard_map/reduce_scatter | solution.py:353
  923.5 142.3 %reduce-scatter.17.cloned.1.call-done = f32[96,768]{1,0:T(8,128)} async-done(((f32[3072,768]{1,0:T(8,128)}), f32[96,768]{1,0:T(8,128)}) %reduce-scatter.17.cloned.1.call-update) | async-done | bytes 294928 | tf_op jit(solution)/shard_map/reduce_scatter | solution.py:356
  1065.8 141.0 %reduce-scatter.15.cloned.1.call-done = f32[96,768]{1,0:T(8,128)} async-done(((f32[3072,768]{1,0:T(8,128)}), f32[96,768]{1,0:T(8,128)}) %reduce-scatter.15.cloned.1.call-update) | async-done | bytes 294928 | tf_op jit(solution)/shard_map/reduce_scatter | solution.py:355
  1206.8 833.8 %reduce-scatter.9.cloned.1.call-done = f32[6144,128]{1,0:T(8,128)} async-done(((f32[196608,128]{1,0:T(8,128)}), f32[6144,128]{1,0:T(8,128)}) %reduce-scatter.9.cloned.1.call-update) | async-done | bytes 3145744 | tf_op jit(solution)/shard_map/reduce_scatter | solution.py:330
  2040.6 1.8 copy.232
  2048.3 2.3 copy.237
  (349 shorter events, 68.2 us)
Async XLA Ops:
  8.0 9.6 copy-start
  8.1 282.0 %all-gather.8.cloned.1.call-start = ((), (), s32[]{:S(2)}) async-start(), calls=%async_computation.6 | async-start | bytes 51904512 | tf_op jit(solution)/shard_map/all_gather | solution.py:284
  8.8 393.8 %reduce-scatter.7.cloned.1.call-start = ((), (), s32[]{:S(2)}) async-start(), calls=%async_computation.7 | async-start | bytes 3538944 | tf_op jit(solution)/shard_map/reduce_scatter | solution.py:291
  13.8 7.5 copy-start.27
  21.3 8.4 copy-start.4
  29.9 286.0 %copy-start.67 = (f32[8,33]{1,0:T(8,128)}, f32[8,33]{1,0:T(8,128)S(1)}, u32[]{:S(2)}) copy-start(f32[8,33]{1,0:T(8,128)S(1)} %multiply_reduce_fusion.14) | copy-start | bytes 3172
  30.2 285.8 %copy-start.57 = (bf16[8,4,128]{2,1,0:T(4,128)(2,1)}, bf16[8,4,128]{2,1,0:T(4,128)(2,1)S(1)}, u32[]{:S(2)}) copy-start(bf16[8,4,128]{2,1,0:T(4,128)(2,1)S(1)} %dynamic-slice_convert_fusion) | copy-start | bytes 24580
  315.9 8.2 copy-start.10
  329.9 76.1 %all-gather.10.cloned.1.call-start = ((), (), s32[]{:S(2)}) async-start(), calls=%async_computation.8 | async-start | bytes 4423680 | tf_op jit(solution)/shard_map/all_gather | solution.py:267
  330.5 75.6 %copy-start.69 = (f32[768]{0:T(1024)S(1)}, f32[768]{0:T(1024)}, u32[]{:S(2)}) copy-start(f32[768]{0:T(1024)} %param.42) | copy-start | bytes 9220
  330.5 88.0 %all-gather.12.cloned.1.call-start = ((), (), s32[]{:S(2)}) async-start(), calls=%async_computation.9 | async-start | bytes 1474560 | tf_op jit(solution)/shard_map/all_gather | solution.py:268
  331.1 91.2 %all-gather.14.cloned.1.call-start = ((), (), s32[]{:S(2)}) async-start(), calls=%async_computation.10 | async-start | bytes 5898240 | tf_op jit(solution)/shard_map/all_gather | solution.py:269
  331.6 125.6 %all-gather.16.cloned.1.call-start = ((), (), s32[]{:S(2)}) async-start(), calls=%async_computation.11 | async-start | bytes 5898240 | tf_op jit(solution)/shard_map/all_gather | solution.py:270
  332.4 215.4 %all-gather.18.cloned.1.call-start = ((), (), s32[]{:S(2)}) async-start(), calls=%async_computation.17 | async-start | bytes 3538944 | tf_op jit(solution)/shard_map/all_gather | solution.py:320
  332.4 73.2 %copy-start.94 = (f32[8,1,128]{2,1,0:T(1,128)}, f32[8,1,128]{2,1,0:T(1,128)S(1)}, u32[]{:S(2)}) copy-start(f32[8,1,128]{2,1,0:T(1,128)S(1)} %slice.33) | copy-start | bytes 12292
  333.1 80.0 %copy-start.95 = (pred[256]{0:T(512)(128)(4,1)}, pred[256]{0:T(512)(128)(4,1)S(1)}, u32[]{:S(2)}) copy-start(pred[256]{0:T(512)(128)(4,1)S(1)} %iota_compare_fusion.1) | copy-start | bytes 772
  333.5 76.8 %copy-start.59 = (f32[768]{0:T(1024)}, f32[768]{0:T(1024)S(1)}, u32[]{:S(2)}) copy-start(f32[768]{0:T(1024)S(1)} %convolution_reduce_fusion) | copy-start | bytes 9220
  406.0 7.2 copy-start.87
  406.0 7.1 copy-start.91
  418.4 9.3 copy-start.39
  457.3 10.8 copy-start.72
  457.3 10.8 copy-start.75
  457.3 10.8 copy-start.83
  457.3 10.8 copy-start.108
  487.1 299.0 %reduce-scatter.13.cloned.1.call-start = ((), (), s32[]{:S(2)}) async-start(), calls=%async_computation.14 | async-start | bytes 2433024 | tf_op jit(solution)/shard_map/reduce_scatter | solution.py:354
  494.3 304.5 %all-reduce.8.cloned.1.call-start = ((), (), s32[]{:S(2)}) async-start(), calls=%async_computation.18 | async-start | bytes 5505024 | tf_op jit(solution)/shard_map/psum | solution.py:360
  575.6 23.1 %copy-start.100 = (f32[128]{0:T(128)S(1)}, f32[128]{0:T(128)}, u32[]{:S(2)}) copy-start(f32[128]{0:T(128)} %param.37) | copy-start | bytes 1540
  575.6 23.8 %copy-start.68 = (f32[8,33]{1,0:T(8,128)S(1)}, f32[8,33]{1,0:T(8,128)}, u32[]{:S(2)}) copy-start(f32[8,33]{1,0:T(8,128)} %copy-done.67) | copy-start | bytes 3172
  575.6 24.1 %copy-start.5 = (f32[8,33,2048]{2,1,0:T(8,128)S(1)}, f32[8,33,2048]{2,1,0:T(8,128)}, u32[]{:S(2)}) copy-start(f32[8,33,2048]{2,1,0:T(8,128)} %copy-done.4) | copy-start | bytes 6488068
  575.6 24.1 %copy-start.8 = (f32[8,33,2048]{2,1,0:T(8,128)S(1)}, f32[8,33,2048]{2,1,0:T(8,128)}, u32[]{:S(2)}) copy-start(f32[8,33,2048]{2,1,0:T(8,128)} %copy-done.7) | copy-start | bytes 6488068
  608.2 8.0 copy-start.64
  609.2 7.9 copy-start.45
  611.2 7.6 copy-start.28
  621.9 6.9 copy-start.44
  635.1 288.3 %reduce-scatter.11.cloned.1.call-start = ((), (), s32[]{:S(2)}) async-start(), calls=%async_computation.13 | async-start | bytes 7299072 | tf_op jit(solution)/shard_map/reduce_scatter | solution.py:353
  640.6 425.2 %reduce-scatter.17.cloned.1.call-start = ((), (), s32[]{:S(2)}) async-start(), calls=%async_computation.16 | async-start | bytes 9732096 | tf_op jit(solution)/shard_map/reduce_scatter | solution.py:356
  653.2 553.6 %reduce-scatter.15.cloned.1.call-start = ((), (), s32[]{:S(2)}) async-start(), calls=%async_computation.15 | async-start | bytes 9732096 | tf_op jit(solution)/shard_map/reduce_scatter | solution.py:355
  660.6 1380.0 %reduce-scatter.9.cloned.1.call-start = ((), (), s32[]{:S(2)}) async-start(), calls=%async_computation.12 | async-start | bytes 103809024 | tf_op jit(solution)/shard_map/reduce_scatter | solution.py:330
  734.8 7.6 copy-start.34
  734.8 7.6 copy-start.53
  734.9 8.6 copy-start.36
  734.9 8.6 copy-start.54
  734.9 10.4 copy-start.104
  734.9 10.4 copy-start.105
  734.9 10.4 copy-start.106
  734.9 10.4 copy-start.107
  742.5 1309.1 %copy-start.1 = (f32[128,2048]{1,0:T(8,128)S(1)}, f32[128,2048]{1,0:T(8,128)}, u32[]{:S(2)}) copy-start(f32[128,2048]{1,0:T(8,128)} %param.34) | copy-start | bytes 3145732
  798.9 1251.7 %copy-start.46 = (f32[2048,128]{1,0:T(8,128)S(1)}, f32[2048,128]{1,0:T(8,128)}, u32[]{:S(2)}) copy-start(f32[2048,128]{1,0:T(8,128)} %get-tuple-element.165) | copy-start | bytes 3145732
  (75 other events, 236.2 us)
Sparse Core Ops, SparseCore 0:
  11.8 278.2 all-gather.7
  330.0 72.5 reduce-scatter.6
  487.3 60.4 all-gather.17
  553.5 97.6 reduce-scatter.12
  659.7 139.0 all-reduce.7
  805.0 118.4 reduce-scatter.10
  931.0 134.7 reduce-scatter.16
  1072.3 134.5 reduce-scatter.14
  1215.0 825.6 reduce-scatter.8
Sparse Core Ops, SparseCore 1:
  331.9 28.7 all-gather.9
  362.2 17.3 all-gather.11
  381.0 37.3 all-gather.13
  419.9 37.3 all-gather.15
where the time goes:
time: 2070 us; the launch traced here: 2060 us
  waiting for transfers between devices  1670 us (81%)
  matrix products  245 us (12%)
  local copies, waits for them, and re-layouts  65.3 us (3%)
  blocking collectives  39.6 us (2%)
  other arithmetic  22.8 us (1%)
    reduce_scatter x1, waiting for transfers between devices, body(): lax.psum_scatter(contract_rows(d_kernel, band_low) * factor, ('band', 'to...  834 us
    all_gather x1, waiting for transfers between devices, body(): gen_full = lax.all_gather(gen_w, ('band', 'tok'), axis=0, tiled=True)  260 us
    reduce_scatter x1, waiting for transfers between devices, body(): lax.psum_scatter(grad_down, ('band', 'tok'), scatter_dimension=0, tiled=T...  142 us
    reduce_scatter x1, waiting for transfers between devices, body(): lax.psum_scatter(up_turned, ('band', 'tok'), scatter_dimension=0, tiled=T...  141 us
    reduce_scatter x1, waiting for transfers between devices, body(): lax.psum_scatter(qkv_turned, ('band', 'tok'), scatter_dimension=0, tiled=...  125 us
    reduce_scatter x1, waiting for transfers between devices, body(): lax.psum_scatter(product.reshape(own_images * slot_count * lax.axis_size(...  69.1 us
    dot_general x5, matrix products, contract_rows(): lax.dot_general(left_side, right_side, (((0,), (0,)), ((), ())), preferre...  66.2 us
    unnamed x232, local copies, waits for them, and re-layouts  54.6 us
  transfers between devices with their start and end apart: 13, of which 9 were waited for; matrix products, arithmetic and copies ran while one was open for 12% of the time, Pallas kernels for 0%

commit v1 on v0

--- a/solution.py
+++ b/solution.py
@@ -317,7 +317,32 @@
     d_bias = jnp.sum(d_embed.reshape(own_images, slot_count, model_dim), axis=1)
     d_bias_feat = jnp.dot(d_bias, gen_b.T, precision=PRECISE)
     grad_gen_b = jnp.dot(bias_own.T, d_bias, precision=PRECISE)
-    d_gathered = lax.all_gather(d_embed_low, "band", axis=0, tiled=True)
+    parts_out, m_next, y1 = (
+        jax.lax.axis_size("band"),
+        jax.lax.axis_index("band"),
+        d_embed_low.shape[0],
+    )
+    parts_seen = [p * parts_out if ii == 0 else p for ii, p in enumerate(d_embed_low.shape)]
+    d_gathered = lax.dynamic_update_slice_in_dim(
+        jnp.zeros(parts_seen, d_embed_low.dtype), d_embed_low, m_next * y1, axis=0
+    )
+    oldest = all_values = d_embed_low
+    for rr in range(1, parts_out // 2 + 1):
+        oldest = jax.lax.ppermute(
+            oldest, axis_name="band", perm=[(ii, (ii + 1) % parts_out) for ii in range(parts_out)]
+        )
+        d_gathered = lax.dynamic_update_slice_in_dim(
+            d_gathered, oldest, (m_next - rr) % parts_out * y1, axis=0
+        )
+        if 2 * rr < parts_out:
+            all_values = jax.lax.ppermute(
+                all_values,
+                axis_name="band",
+                perm=[(ii, (ii - 1) % parts_out) for ii in range(parts_out)],
+            )
+            d_gathered = lax.dynamic_update_slice_in_dim(
+                d_gathered, all_values, (m_next + rr) % parts_out * y1, axis=0
+            )
     pixel_grad = jnp.einsum(
         "isd,ibpd->ibsp", d_gathered, kernel_grid, preferred_element_type=jnp.float32
     ).astype(jnp.bfloat16)[None]

time: 2070 us -> 2170 us (1.048)
  waiting for transfers between devices: 1670 us -> 1720 us
  local copies, waits for them, and re-layouts: 65.3 us -> 95.2 us
    reduce_scatter x1, waiting for transfers between devices: 0.01 us -> 92.9 us  [body(): lax.psum_scatter(out_turned, ('band', 'tok'), scatter_dimension=0, tiled=...]
    all_gather x1 -> x0, waiting for transfers between devices: 51.9 us -> none  [body(): d_gathered = lax.all_gather(d_embed_low, 'band', axis=0, tiled=True)]
    ppermute x0 -> x7, waiting for transfers between devices: none -> 25.2 us  [the longest x4 25.2 us: body(): jax.lax.ppermute(oldest, axis_name='band', perm=[(ii, (ii + 1) % parts_ou...]
    unnamed x232 -> x226, local copies, waits for them, and re-layouts: 54.6 us -> 52.4 us
  transfers between devices with their start and end apart: 13 -> 19, of which waited for: 9 -> 10; matrix products, arithmetic and copies ran while one was open for 12% -> 9% of each run, Pallas kernels for 0% -> 0%
where the time goes in v1:
time: 2170 us; the launch traced here: 2160 us
  waiting for transfers between devices  1720 us (79%)
  matrix products  242 us (11%)
  local copies, waits for them, and re-layouts  95.2 us (4%)
  blocking collectives  39.7 us (2%)
  other arithmetic  23.4 us (1%)
    reduce_scatter x1, waiting for transfers between devices, body(): lax.psum_scatter(contract_rows(d_kernel, band_low) * factor, ('band', 'to...  834 us
    all_gather x1, waiting for transfers between devices, body(): gen_full = lax.all_gather(gen_w, ('band', 'tok'), axis=0, tiled=True)  260 us
    reduce_scatter x1, waiting for transfers between devices, body(): lax.psum_scatter(grad_down, ('band', 'tok'), scatter_dimension=0, tiled=T...  142 us
    reduce_scatter x1, waiting for transfers between devices, body(): lax.psum_scatter(up_turned, ('band', 'tok'), scatter_dimension=0, tiled=T...  141 us
    reduce_scatter x1, waiting for transfers between devices, body(): lax.psum_scatter(qkv_turned, ('band', 'tok'), scatter_dimension=0, tiled=...  124 us
    reduce_scatter x1, waiting for transfers between devices, body(): lax.psum_scatter(out_turned, ('band', 'tok'), scatter_dimension=0, tiled=...  92.9 us
    reduce_scatter x1, waiting for transfers between devices, body(): lax.psum_scatter(product.reshape(own_images * slot_count * lax.axis_size(...  69.3 us
    dot_general x5, matrix products, contract_rows(): lax.dot_general(left_side, right_side, (((0,), (0,)), ((), ())), preferre...  64.8 us
  transfers between devices with their start and end apart: 19, of which 10 were waited for; matrix products, arithmetic and copies ran while one was open for 9% of the time, Pallas kernels for 0%

profile of v1, /device:TPU:0, one launch (start us, length us, event | category | flops | bytes accessed | tf_op | source)
XLA Modules:
  0.0 2155.9 jit_solution(16485216137974787060)
XLA Ops:
  17.6 3.6 fusion.85
  21.3 6.0 fusion.27
  27.3 2.4 fusion.208
  30.2 259.9 %all-gather.6.cloned.1.call-done = bf16[196608,128]{1,0:T(8,128)(2,1)} async-done(((bf16[6144,128]{1,0:T(8,128)(2,1)}), bf16[196608,128]{1,0:T(8,128)(2,1)}) %all-gather.6.cloned.1.call-update) | async-done | bytes 50331664 | tf_op jit(solution)/shard_map/all_gather | solution.py:284
  290.0 25.9 %fusion.1 = bf16[32,196608]{1,0:T(8,128)(2,1)} fusion(bf16[32,128]{1,0:T(8,128)(2,1)S(1)} %bitcast.313, bf16[196608,128]{1,0:T(8,128)(2,1)} %all-gather.6.cloned.1.call-done), kind=kOutput, calls=%fused_computation.3 | convolution fusion | flops 1623195648 | bytes 62922752 | tf_op jit(solution)/shard_map/dot_general | solution.py:93
  315.9 8.2 copy.243
  324.1 5.7 bitcast_convert_fusion
  333.5 69.3 %reduce-scatter.7.cloned.1.call-done = bf16[256,768]{1,0:T(8,128)(2,1)} async-done(((bf16[2048,768]{1,0:T(8,128)(2,1)}), bf16[256,768]{1,0:T(8,128)(2,1)}) %reduce-scatter.7.cloned.1.call-update) | async-done | bytes 393232 | tf_op jit(solution)/shard_map/reduce_scatter | solution.py:291
  406.2 4.2 convolution_convert_fusion
  410.4 2.9 copy.179
  418.6 2.0 fusion.212
  422.4 5.5 fusion.200
  427.8 29.4 %all-gather.14.cloned.1.call-done = bf16[3072,768]{1,0:T(8,128)(2,1)} async-done(((bf16[768,768]{1,0:T(8,128)(2,1)}), bf16[3072,768]{1,0:T(8,128)(2,1)}) %all-gather.14.cloned.1.call-update) | async-done | bytes 4718608 | tf_op jit(solution)/shard_map/all_gather | solution.py:270
  457.3 10.7 add_convert_fusion
  468.1 2.3 multiply_reduce_fusion.1
  475.0 2.8 fusion.67
  488.6 3.2 collective-permute-start.1
  491.8 14.3 collective-permute-done
  506.1 2.5 collective-permute-start.2
  509.4 2.8 collective-permute-start.3
  514.4 10.9 collective-permute-done.2
  525.3 2.5 collective-permute-start.4
  536.8 2.8 collective-permute-start.5
  563.7 11.1 convert_bitcast_fusion
  574.7 16.6 copy.244
  591.4 22.4 %convolution_multiply_fusion.5 = f32[32,128]{1,0:T(8,128)S(1)} fusion(bf16[32,196608]{1,0:T(8,128)(2,1)} %bitcast.277, bf16[196608,128]{1,0:T(8,128)(2,1)} %all-gather.6.cloned.1.call-done), kind=kOutput, calls=%fused_computation.126 | convolution fusion | flops 1610616832 | bytes 62930944 | tf_op jit(solution)/shard_map/dot_general | solution.py:354
  616.3 6.3 convolution_bitcast_fusion
  622.6 3.2 multiply_add_fusion
  625.8 2.4 multiply_reduce_fusion.12
  628.2 3.4 convolution_bitcast_fusion.1
  635.3 2.2 copy.196
  637.5 2.7 multiply_reduce_fusion.9
  640.2 2.0 fusion.197
  652.1 5.4 fusion.92
  658.5 11.6 fusion.39
  670.8 6.7 fusion.199
  678.2 39.2 %convolution_multiply_fusion = f32[196608,128]{1,0:T(8,128)} fusion(bf16[32,196608]{1,0:T(8,128)(2,1)} %bitcast.278, bf16[32,128]{1,0:T(8,128)(2,1)S(1)} %bitcast.314), kind=kOutput, calls=%fused_computation.1 | convolution fusion | flops 1635778560 | bytes 113254400 | tf_op jit(solution)/shard_map/dot_general | solution.py:87
  718.4 3.2 convolution_convert_fusion.1
  726.8 13.5 fusion.70
  740.3 11.3 convert_bitcast_fusion.1
  751.7 6.6 copy.211
  762.0 39.7 %all-reduce.4 = (f32[128]{0:T(128)}, f32[128]{0:T(128)}, f32[128]{0:T(128)}, f32[768]{0:T(1024)S(1)}, f32[768]{0:T(1024)S(1)}) all-reduce(f32[128]{0:T(128)S(1)} %fusion.153, f32[128]{0:T(128)S(1)} %copy-done.104, f32[128]{0:T(128)S(1)} %copy-done.103, f32[768]{0:T(1024)S(1)} %copy-done.102, ...), channel_id=1, replica_groups=mesh['band'=8,'tok'=4] {'band','tok'}, use_global_device_ids=true, to_apply=%region_34.35 | all-reduce | flops 1920 | bytes 15360 | tf_op jit(solution)/shard_map/psum | solution.py:385
  802.9 92.9 %reduce-scatter.13.cloned.1.call-done = f32[24,768]{1,0:T(8,128)} async-done(((f32[768,768]{1,0:T(8,128)}), f32[24,768]{1,0:T(8,128)}) %reduce-scatter.13.cloned.1.call-update) | async-done | bytes 73744 | tf_op jit(solution)/shard_map/reduce_scatter | solution.py:379
  895.8 124.2 %reduce-scatter.11.cloned.1.call-done = f32[72,768]{1,0:T(8,128)} async-done(((f32[2304,768]{1,0:T(8,128)}), f32[72,768]{1,0:T(8,128)}) %reduce-scatter.11.cloned.1.call-update) | async-done | bytes 221200 | tf_op jit(solution)/shard_map/reduce_scatter | solution.py:378
  1020.0 142.3 %reduce-scatter.17.cloned.1.call-done = f32[96,768]{1,0:T(8,128)} async-done(((f32[3072,768]{1,0:T(8,128)}), f32[96,768]{1,0:T(8,128)}) %reduce-scatter.17.cloned.1.call-update) | async-done | bytes 294928 | tf_op jit(solution)/shard_map/reduce_scatter | solution.py:381
  1162.2 141.1 %reduce-scatter.15.cloned.1.call-done = f32[96,768]{1,0:T(8,128)} async-done(((f32[3072,768]{1,0:T(8,128)}), f32[96,768]{1,0:T(8,128)}) %reduce-scatter.15.cloned.1.call-update) | async-done | bytes 294928 | tf_op jit(solution)/shard_map/reduce_scatter | solution.py:380
  1303.3 833.9 %reduce-scatter.9.cloned.1.call-done = f32[6144,128]{1,0:T(8,128)} async-done(((f32[196608,128]{1,0:T(8,128)}), f32[6144,128]{1,0:T(8,128)}) %reduce-scatter.9.cloned.1.call-update) | async-done | bytes 3145744 | tf_op jit(solution)/shard_map/reduce_scatter | solution.py:355
  2144.8 2.3 copy.277
  (371 shorter events, 111.9 us)
Async XLA Ops:
  8.0 9.6 copy-start
  8.1 282.0 %all-gather.6.cloned.1.call-start = ((), (), s32[]{:S(2)}) async-start(), calls=%async_computation.6 | async-start | bytes 51904512 | tf_op jit(solution)/shard_map/all_gather | solution.py:284
  8.8 394.0 %reduce-scatter.7.cloned.1.call-start = ((), (), s32[]{:S(2)}) async-start(), calls=%async_computation.7 | async-start | bytes 3538944 | tf_op jit(solution)/shard_map/reduce_scatter | solution.py:291
  21.3 8.4 copy-start.4
  29.9 286.0 %copy-start.65 = (f32[8,33]{1,0:T(8,128)}, f32[8,33]{1,0:T(8,128)S(1)}, u32[]{:S(2)}) copy-start(f32[8,33]{1,0:T(8,128)S(1)} %multiply_reduce_fusion.14) | copy-start | bytes 3172
  30.2 285.8 %copy-start.54 = (bf16[8,4,128]{2,1,0:T(4,128)(2,1)}, bf16[8,4,128]{2,1,0:T(4,128)(2,1)S(1)}, u32[]{:S(2)}) copy-start(bf16[8,4,128]{2,1,0:T(4,128)(2,1)S(1)} %dynamic-slice_convert_fusion) | copy-start | bytes 24580
  329.9 76.3 %all-gather.8.cloned.1.call-start = ((), (), s32[]{:S(2)}) async-start(), calls=%async_computation.8 | async-start | bytes 4423680 | tf_op jit(solution)/shard_map/all_gather | solution.py:267
  330.5 75.7 %copy-start.67 = (f32[768]{0:T(1024)S(1)}, f32[768]{0:T(1024)}, u32[]{:S(2)}) copy-start(f32[768]{0:T(1024)} %param.42) | copy-start | bytes 9220
  330.5 88.1 %all-gather.10.cloned.1.call-start = ((), (), s32[]{:S(2)}) async-start(), calls=%async_computation.9 | async-start | bytes 1474560 | tf_op jit(solution)/shard_map/all_gather | solution.py:268
  331.1 91.3 %all-gather.12.cloned.1.call-start = ((), (), s32[]{:S(2)}) async-start(), calls=%async_computation.10 | async-start | bytes 5898240 | tf_op jit(solution)/shard_map/all_gather | solution.py:269
  331.6 125.6 %all-gather.14.cloned.1.call-start = ((), (), s32[]{:S(2)}) async-start(), calls=%async_computation.11 | async-start | bytes 5898240 | tf_op jit(solution)/shard_map/all_gather | solution.py:270
  332.4 470.5 %all-reduce.8.cloned.1.call-start = ((), (), s32[]{:S(2)}) async-start(), calls=%async_computation.17 | async-start | bytes 5505024 | tf_op jit(solution)/shard_map/psum | solution.py:385
  332.4 73.3 %copy-start.91 = (f32[8,1,128]{2,1,0:T(1,128)}, f32[8,1,128]{2,1,0:T(1,128)S(1)}, u32[]{:S(2)}) copy-start(f32[8,1,128]{2,1,0:T(1,128)S(1)} %slice.33) | copy-start | bytes 12292
  333.1 80.1 %copy-start.92 = (pred[256]{0:T(512)(128)(4,1)}, pred[256]{0:T(512)(128)(4,1)S(1)}, u32[]{:S(2)}) copy-start(pred[256]{0:T(512)(128)(4,1)S(1)} %iota_compare_fusion.1) | copy-start | bytes 772
  333.5 76.9 %copy-start.56 = (f32[768]{0:T(1024)}, f32[768]{0:T(1024)S(1)}, u32[]{:S(2)}) copy-start(f32[768]{0:T(1024)S(1)} %convolution_reduce_fusion) | copy-start | bytes 9220
  418.5 9.3 copy-start.36
  457.3 10.8 copy-start.70
  457.3 10.8 copy-start.73
  457.3 10.8 copy-start.80
  457.3 10.8 copy-start.105
  485.1 23.5 %copy-start.61 = (f32[8,4,33]{2,1,0:T(4,128)S(1)}, f32[8,4,33]{2,1,0:T(4,128)}, u32[]{:S(2)}) copy-start(f32[8,4,33]{2,1,0:T(4,128)} %copy-done.60) | copy-start | bytes 12676
  487.1 19.0 collective-permute-start
  488.6 20.8 collective-permute-start.1
  506.1 19.2 collective-permute-start.2
  509.4 27.4 %collective-permute-start.3 = (bf16[1,256,768]{2,1,0:T(8,128)(2,1)}, bf16[1,256,768]{2,1,0:T(8,128)(2,1)}, u32[]{:S(2)}, u32[]{:S(2)}) collective-permute-start(bf16[1,256,768]{2,1,0:T(8,128)(2,1)} %collective-permute-done.1), channel_id=1, source_target_pairs={{0,28},{4,0},{8,4},{12,8},{16,12},{20,16},{24,20},{28,24},{1,29},{... | collective-permute-start | bytes 1179656 | tf_op jit(solution)/shard_map/ppermute | solution.py:338
  525.3 21.6 %collective-permute-start.4 = (bf16[1,256,768]{2,1,0:T(8,128)(2,1)}, bf16[1,256,768]{2,1,0:T(8,128)(2,1)}, u32[]{:S(2)}, u32[]{:S(2)}) collective-permute-start(bf16[1,256,768]{2,1,0:T(8,128)(2,1)} %collective-permute-done.2), channel_id=1, source_target_pairs={{0,4},{4,8},{8,12},{12,16},{16,20},{20,24},{24,28},{28,0},{1,5},{5... | collective-permute-start | bytes 1179656 | tf_op jit(solution)/shard_map/ppermute | solution.py:331
  536.8 17.7 collective-permute-start.5
  547.0 13.0 collective-permute-start.6
  591.4 22.5 %copy-start.97 = (f32[128]{0:T(128)S(1)}, f32[128]{0:T(128)}, u32[]{:S(2)}) copy-start(f32[128]{0:T(128)} %param.37) | copy-start | bytes 1540
  591.4 23.9 %copy-start.66 = (f32[8,33]{1,0:T(8,128)S(1)}, f32[8,33]{1,0:T(8,128)}, u32[]{:S(2)}) copy-start(f32[8,33]{1,0:T(8,128)} %copy-done.65) | copy-start | bytes 3172
  591.4 24.9 %copy-start.5 = (f32[8,33,2048]{2,1,0:T(8,128)S(1)}, f32[8,33,2048]{2,1,0:T(8,128)}, u32[]{:S(2)}) copy-start(f32[8,33,2048]{2,1,0:T(8,128)} %copy-done.4) | copy-start | bytes 6488068
  591.4 24.9 %copy-start.7 = (f32[8,33,2048]{2,1,0:T(8,128)S(1)}, f32[8,33,2048]{2,1,0:T(8,128)}, u32[]{:S(2)}) copy-start(f32[8,33,2048]{2,1,0:T(8,128)} %copy-done.6) | copy-start | bytes 6488068
  628.2 9.3 copy-start.17
  631.6 8.6 copy-start.62
  632.6 9.6 copy-start.41
  649.8 245.9 %reduce-scatter.13.cloned.1.call-start = ((), (), s32[]{:S(2)}) async-start(), calls=%async_computation.14 | async-start | bytes 2433024 | tf_op jit(solution)/shard_map/reduce_scatter | solution.py:379
  651.8 368.1 %reduce-scatter.11.cloned.1.call-start = ((), (), s32[]{:S(2)}) async-start(), calls=%async_computation.13 | async-start | bytes 7299072 | tf_op jit(solution)/shard_map/reduce_scatter | solution.py:378
  657.5 504.7 %reduce-scatter.17.cloned.1.call-start = ((), (), s32[]{:S(2)}) async-start(), calls=%async_computation.16 | async-start | bytes 9732096 | tf_op jit(solution)/shard_map/reduce_scatter | solution.py:381
  670.2 633.1 %reduce-scatter.15.cloned.1.call-start = ((), (), s32[]{:S(2)}) async-start(), calls=%async_computation.15 | async-start | bytes 9732096 | tf_op jit(solution)/shard_map/reduce_scatter | solution.py:380
  677.5 1459.7 %reduce-scatter.9.cloned.1.call-start = ((), (), s32[]{:S(2)}) async-start(), calls=%async_computation.12 | async-start | bytes 103809024 | tf_op jit(solution)/shard_map/reduce_scatter | solution.py:355
  751.6 8.6 copy-start.32
  751.6 8.6 copy-start.51
  751.6 10.4 copy-start.101
  751.6 10.4 copy-start.102
  751.6 10.4 copy-start.103
  751.6 10.4 copy-start.104
  759.2 1388.9 %copy-start.1 = (f32[128,2048]{1,0:T(8,128)S(1)}, f32[128,2048]{1,0:T(8,128)}, u32[]{:S(2)}) copy-start(f32[128,2048]{1,0:T(8,128)} %param.34) | copy-start | bytes 3145732
  802.9 1344.2 %copy-start.42 = (f32[2048,128]{1,0:T(8,128)S(1)}, f32[2048,128]{1,0:T(8,128)}, u32[]{:S(2)}) copy-start(f32[2048,128]{1,0:T(8,128)} %get-tuple-element.165) | copy-start | bytes 3145732
  (78 other events, 251.2 us)
Sparse Core Ops, SparseCore 0:
  11.8 278.2 all-gather.5
  330.0 72.7 reduce-scatter.6
  649.9 140.9 all-reduce.7
  797.5 98.2 reduce-scatter.12
  901.9 118.0 reduce-scatter.10
  1027.3 134.8 reduce-scatter.16
  1168.7 134.5 reduce-scatter.14
  1311.4 825.6 reduce-scatter.8
Sparse Core Ops, SparseCore 1:
  331.9 28.7 all-gather.7
  362.2 17.3 all-gather.9
  381.0 37.3 all-gather.11
  419.9 37.3 all-gather.13
